TPU v7x, 256 devices: a whole 4x4x8 slice. The times are simulated.
256 devices in a mesh: view: 8 (over y, x_lo), band: 32 (over x_hi, z, core).
Axes of the slice: x: 4 (x_hi: 2, x_lo: 2; x = x_hi * 2 + x_lo), y: 4, z: 8, core: 2. Of those that a mesh axis runs over, the one named last changes fastest.
Arguments:
- features: float32 [8, 256, 512, 128], P('view', 'band'), may hold values from -6 to 6
- tempers: float32 [8, 256, 512], P('view', 'band'), may hold values from 0.5 to 80
- partners: int32 [8, 2], replicated, may hold values from 0 to 7, as said below
- conv_one: bfloat16 [3, 3, 128, 128], replicated, may hold values from -0.1875 to 0.1875
- conv_two: bfloat16 [3, 3, 128, 128], replicated, may hold values from -0.1875 to 0.1875
- query_weight: bfloat16 [128, 128], replicated, may hold values from -0.5 to 0.5
- key_weight: bfloat16 [128, 128], replicated, may hold values from -0.5 to 0.5
- value_weight: bfloat16 [128, 128], replicated, may hold values from -0.5 to 0.5
- out_weight: bfloat16 [128, 128], replicated, may hold values from -0.5 to 0.5
- norm_gain: float32 [128], replicated, may hold values from 0.25 to 1.75
- message_gain: float32 [128], replicated, may hold values from 0.25 to 1.75
Outputs:
- refined: float32 [8, 256, 512, 128], P('view', 'band')
Inputs may be any that keep to these rules, and one draw needn't show every extreme that they name: Column 0 and column 1 are each a permutation of the 8 views; a view is never its own partner, and its two partners differ. At least one view has as its first partner the view 4 positions away from it (modulo 8).
All inputs are finite; a program needn't handle non-finite values.
Results may differ from a plain program's by a relative error of at most 0.0065.
Values may be sent and summed in bfloat16 or wider, within the bound.
A program may use at most 64 MiB of HBM per device.

v0:
```python
import math

import jax
import jax.numpy as jnp
from jax import lax
from jax.sharding import PartitionSpec as P

epsilon = 1e-06


def extended(cells, sides, width):
    for axis, dim in sides:
        count = lax.axis_size(axis)
        ends = count - 1
        head = lax.slice_in_dim(cells, 0, width, axis=dim)
        tail = lax.slice_in_dim(cells, cells.shape[dim] - width, cells.shape[dim], axis=dim)
        cells = jnp.concatenate(
            [
                lax.ppermute(tail, axis, [(i, (i + 1) % count) for i in range(ends)]),
                cells,
                lax.ppermute(head, axis, [((i + 1) % count, i) for i in range(ends)]),
            ],
            axis=dim,
        )
    return cells


def root_norm(values, gain):
    mean_square = jnp.mean(values * values, axis=-1, keepdims=True)
    return values * lax.rsqrt(mean_square + epsilon) * gain


def convolve(padded, kernel):
    leading = padded.shape[:-3]
    out_rows = padded.shape[-3] - 2
    columns = padded.shape[-2]
    channels = padded.shape[-1]
    widened = jnp.pad(padded, [(0, 0)] * len(leading) + [(0, 0), (1, 1), (0, 0)])
    summed = jnp.zeros(leading + (out_rows, columns, kernel.shape[-1]), jnp.float32)
    for row_tap in range(3):
        for col_tap in range(3):
            window = widened[..., row_tap : row_tap + out_rows, col_tap : col_tap + columns, :]
            product = jnp.dot(
                window.reshape(-1, channels),
                kernel[row_tap, col_tap],
                preferred_element_type=jnp.float32,
            )
            summed = summed + product.reshape(summed.shape)
    return summed


def route_pair(normed_rows, own_view, partners):
    every_view = lax.all_gather(normed_rows[None], "view", axis=0, tiled=True)
    chosen = lax.dynamic_index_in_dim(partners, own_view, 0, keepdims=False)
    return jnp.take(every_view, chosen, axis=0)


def per_device(
    features,
    tempers,
    partners,
    conv_one,
    conv_two,
    query_weight,
    key_weight,
    value_weight,
    out_weight,
    norm_gain,
    message_gain,
):
    current = features[0]
    temper = tempers[0]
    row_count, columns, channels = current.shape
    first_input = jax.nn.silu(current).astype(jnp.bfloat16)
    first_rows = extended(first_input, (("band", 0),), 1)
    state_one = current + convolve(first_rows, conv_one)
    second_input = jax.nn.silu(state_one).astype(jnp.bfloat16)
    second_rows = extended(second_input, (("band", 0),), 1)
    state_two = state_one + convolve(second_rows, conv_two)
    normed = root_norm(state_two, norm_gain).astype(jnp.bfloat16)
    flat_normed = normed.reshape(-1, channels)
    queries = (
        jnp.dot(flat_normed, query_weight, preferred_element_type=jnp.float32)
        .astype(jnp.bfloat16)
        .reshape(normed.shape)
    )
    own_view = lax.axis_index("view")
    paired = route_pair(normed, own_view, partners)
    paired_rows = extended(paired, (("band", 1),), 1)
    pair_flat = paired_rows.reshape(-1, channels)
    key_rows = (
        jnp.dot(pair_flat, key_weight, preferred_element_type=jnp.float32)
        .astype(jnp.bfloat16)
        .reshape(paired_rows.shape)
    )
    value_rows = (
        jnp.dot(pair_flat, value_weight, preferred_element_type=jnp.float32)
        .astype(jnp.bfloat16)
        .reshape(paired_rows.shape)
    )
    block_size = min(columns, 512)
    factor = 1.0 / math.sqrt(channels)

    def attend_row(row_index):
        query_row = lax.dynamic_index_in_dim(queries, row_index, 0, keepdims=False)
        temper_row = lax.dynamic_index_in_dim(temper, row_index, 0, keepdims=False) * factor
        key_window = lax.dynamic_slice_in_dim(key_rows, row_index, 3, 1).reshape(
            2, 3 * columns, channels
        )
        value_window = lax.dynamic_slice_in_dim(value_rows, row_index, 3, 1).reshape(
            2, 3 * columns, channels
        )
        summed = jnp.zeros((columns, channels), jnp.float32)
        for partner in range(2):
            scores = lax.dot_general(
                query_row,
                key_window[partner],
                (((1,), (1,)), ((), ())),
                preferred_element_type=jnp.float32,
            )
            scores = scores * temper_row[0:block_size, None]
            row_peak = jnp.max(scores, axis=-1, keepdims=True)
            lifted = jnp.exp(scores - row_peak)
            shares = (lifted / jnp.sum(lifted, axis=-1, keepdims=True)).astype(jnp.bfloat16)
            pieces = [
                jnp.dot(shares, value_window[partner], preferred_element_type=jnp.float32).astype(
                    jnp.bfloat16
                )
            ]
            blended = jnp.concatenate(pieces, axis=0)
            summed = summed + jnp.dot(blended, out_weight, preferred_element_type=jnp.float32)
        return summed

    messages = lax.map(attend_row, jnp.arange(row_count, dtype=jnp.int32))
    refined = state_two + root_norm(messages, message_gain)
    return refined[None]


def solution(mesh):
    in_specs = (
        P("view", "band", None, None),
        P("view", "band", None),
        P(),
        P(),
        P(),
        P(),
        P(),
        P(),
        P(),
        P(),
        P(),
    )
    out_specs = P("view", "band", None, None)
    return jax.shard_map(
        per_device, mesh=mesh, in_specs=in_specs, out_specs=out_specs, check_vma=False
    )
```

profile of v0, /device:TPU:6, one launch (start us, length us, event | category | flops | bytes accessed | tf_op | source)
XLA Modules:
  0.0 379.8 jit_solution(6802062921291044743)
XLA Ops:
  6.5 2.3 fusion.19
  8.9 1.9 collective-permute-start
  10.8 8.0 %collective-permute-start.1 = (bf16[1,512,128]{2,1,0:T(8,128)(2,1)S(1)}, bf16[1,512,128]{2,1,0:T(8,128)(2,1)S(1)}, u32[]{:S(2)}, u32[]{:S(2)}) collective-permute-start(bf16[1,512,128]{2,1,0:T(8,128)(2,1)S(1)} %get-tuple-element.79), channel_id=1, source_target_pairs={{1,0},{2,1},{3,2},{4,3},{5,4},{6,5},{7,6},{8,7},{9,8},{10,9},{11,1... | collective-permute-start | bytes 393224 | tf_op jit(solution)/shard_map/ppermute | solution.py:21
  19.6 1.8 collective-permute-done.1
  24.7 1.5 multiply_convert_fusion.1
  26.2 1.9 collective-permute-start.2
  28.2 7.4 %collective-permute-start.3 = (bf16[1,512,128]{2,1,0:T(8,128)(2,1)S(1)}, bf16[1,512,128]{2,1,0:T(8,128)(2,1)S(1)}, u32[]{:S(2)}, u32[]{:S(2)}) collective-permute-start(bf16[1,512,128]{2,1,0:T(8,128)(2,1)S(1)} %get-tuple-element.77), channel_id=1, source_target_pairs={{1,0},{2,1},{3,2},{4,3},{5,4},{6,5},{7,6},{8,7},{9,8},{10,9},{11,1... | collective-permute-start | bytes 393224 | tf_op jit(solution)/shard_map/ppermute | solution.py:21
  36.3 1.8 collective-permute-done.3
  41.4 1.3 multiply_reduce_fusion.1
  42.7 1.3 copy-done.2
  44.0 1.5 multiply_convert_fusion
  45.8 169.9 %all-gather.3.cloned.1.call-done = bf16[64,512,128]{2,1,0:T(8,128)(2,1)} async-done(((bf16[8,512,128]{2,1,0:T(8,128)(2,1)}), bf16[64,512,128]{2,1,0:T(8,128)(2,1)}) %all-gather.3.cloned.1.call-update) | async-done | bytes 8388624 | tf_op jit(solution)/shard_map/all_gather | solution.py:53
  215.7 4.3 %gather_fusion = bf16[2,8,512,128]{3,2,1,0:T(8,128)(2,1)S(1)} fusion(bf16[8,8,512,128]{3,2,1,0:T(8,128)(2,1)} %bitcast.194, s32[1024]{0:T(1024)S(1)} %pad_clamp_fusion), kind=kCustom, calls=%fused_computation | custom fusion | bytes 4194312 | tf_op jit(solution)/shard_map/jit(_take)/gather | solution.py:55
  220.4 1.9 collective-permute-start.4
  222.3 7.4 %collective-permute-start.5 = (bf16[2,1,512,128]{3,2,1,0:T(8,128)(2,1)S(1)}, bf16[2,1,512,128]{3,2,1,0:T(8,128)(2,1)S(1)}, u32[]{:S(2)}, u32[]{:S(2)}) collective-permute-start(bf16[2,1,512,128]{3,2,1,0:T(8,128)(2,1)S(1)} %get-tuple-element.75), channel_id=1, source_target_pairs={{1,0},{2,1},{3,2},{4,3},{5,4},{6,5},{7,6},{8,7},{9,8},{10,9},{11,1... | collective-permute-start | bytes 786440 | tf_op jit(solution)/shard_map/ppermute | solution.py:21
  229.8 1.4 convolution_convert_fusion.2
  231.7 1.8 collective-permute-done.5
  233.8 2.3 convolution_convert_fusion
  236.1 2.3 convolution_convert_fusion.1
  238.5 129.1 %while.10 = (s32[]{:T(128)}, f32[8,512,128]{2,1,0:T(8,128)}, s32[8]{0:T(128)S(1)}, bf16[8,512,128]{2,1,0:T(8,128)(2,1)}, bf16[2,10,512,128]{3,2,1,0:T(8,128)(2,1...) while((s32[]{:T(128)}, f32[8,512,128]{2,1,0:T(8,128)}, ...), condition=%wide.region_6.7_spmd, body=%wide.region_1.0_spmd.sunk | while | flops 850065920 | bytes 26308876 | solution.py:134
  241.8 0.7 dynamic-slice_multiply_fusion.2
  242.5 2.4 constant_dynamic-slice_fusion.5
  244.9 1.6 fusion.146
  247.0 2.6 fusion.148
  249.6 1.6 fusion.149
  252.1 2.5 fusion.151
  257.9 0.7 dynamic-slice_multiply_fusion.2
  258.7 2.4 constant_dynamic-slice_fusion.5
  261.0 1.6 fusion.146
  263.2 2.6 fusion.148
  265.7 1.6 fusion.149
  268.3 2.5 fusion.151
  274.8 2.4 constant_dynamic-slice_fusion.5
  277.2 1.6 fusion.146
  279.3 2.5 fusion.148
  281.9 1.6 fusion.149
  284.4 2.5 fusion.151
  291.0 2.4 constant_dynamic-slice_fusion.5
  293.3 1.6 fusion.146
  295.5 2.6 fusion.148
  298.0 1.6 fusion.149
  300.6 2.5 fusion.151
  307.1 2.4 constant_dynamic-slice_fusion.5
  309.5 1.6 fusion.146
  311.6 2.6 fusion.148
  314.2 1.6 fusion.149
  316.7 2.5 fusion.151
  323.2 2.4 constant_dynamic-slice_fusion.5
  325.6 1.6 fusion.146
  327.7 2.6 fusion.148
  330.3 1.6 fusion.149
  332.9 2.5 fusion.151
  339.4 2.4 constant_dynamic-slice_fusion.5
  341.7 1.6 fusion.146
  343.9 2.6 fusion.148
  346.4 1.6 fusion.149
  349.0 2.5 fusion.151
  355.5 2.4 constant_dynamic-slice_fusion.5
  357.9 1.6 fusion.146
  360.0 2.6 fusion.148
  362.5 1.6 fusion.149
  365.1 2.5 fusion.151
  367.6 2.4 multiply_reduce_fusion
  370.0 2.9 add_bitcast_fusion
  (107 shorter events, 30.8 us)
Async XLA Ops:
  6.5 227.2 %copy-start = (bf16[128,128]{1,0:T(8,128)(2,1)S(1)}, bf16[128,128]{1,0:T(8,128)(2,1)}, u32[]{:S(2)}) copy-start(bf16[128,128]{1,0:T(8,128)(2,1)} %param.20) | copy-start | bytes 98308
  6.5 12.3 %copy-start.6 = (f32[1,8,512,128]{3,2,1,0:T(8,128)S(1)}, f32[1,8,512,128]{3,2,1,0:T(8,128)}, u32[]{:S(2)}) copy-start(f32[1,8,512,128]{3,2,1,0:T(8,128)} %param.13) | copy-start | bytes 6291460
  6.5 12.3 %copy-start.8 = (bf16[3,3,128,128]{3,2,1,0:T(8,128)(2,1)S(1)}, bf16[3,3,128,128]{3,2,1,0:T(8,128)(2,1)}, u32[]{:S(2)}) copy-start(bf16[3,3,128,128]{3,2,1,0:T(8,128)(2,1)} %param.16) | copy-start | bytes 884740
  6.5 209.2 %all-gather.3.cloned.1.call-start = ((), (), s32[]{:S(2)}) async-start(), calls=%async_computation | async-start | bytes 9437184 | tf_op jit(solution)/shard_map/all_gather | solution.py:53
  8.9 10.7 %collective-permute-start = (bf16[1,512,128]{2,1,0:T(8,128)(2,1)S(1)}, bf16[1,512,128]{2,1,0:T(8,128)(2,1)S(1)}, u32[]{:S(2)}, u32[]{:S(2)}) collective-permute-start(bf16[1,512,128]{2,1,0:T(8,128)(2,1)S(1)} %get-tuple-element.78), channel_id=1, source_target_pairs={{0,1},{1,2},{2,3},{3,4},{4,5},{5,6},{6,7},{7,8},{8,9},{9,10},{10,1... | collective-permute-start | bytes 393224 | tf_op jit(solution)/shard_map/ppermute | solution.py:19
  10.8 10.6 %collective-permute-start.1 = (bf16[1,512,128]{2,1,0:T(8,128)(2,1)S(1)}, bf16[1,512,128]{2,1,0:T(8,128)(2,1)S(1)}, u32[]{:S(2)}, u32[]{:S(2)}) collective-permute-start(bf16[1,512,128]{2,1,0:T(8,128)(2,1)S(1)} %get-tuple-element.79), channel_id=1, source_target_pairs={{1,0},{2,1},{3,2},{4,3},{5,4},{6,5},{7,6},{8,7},{9,8},{10,9},{11,1... | collective-permute-start | bytes 393224 | tf_op jit(solution)/shard_map/ppermute | solution.py:21
  24.7 10.9 %copy-start.7 = (bf16[3,3,128,128]{3,2,1,0:T(8,128)(2,1)S(1)}, bf16[3,3,128,128]{3,2,1,0:T(8,128)(2,1)}, u32[]{:S(2)}) copy-start(bf16[3,3,128,128]{3,2,1,0:T(8,128)(2,1)} %param.17) | copy-start | bytes 884740
  26.2 10.0 %collective-permute-start.2 = (bf16[1,512,128]{2,1,0:T(8,128)(2,1)S(1)}, bf16[1,512,128]{2,1,0:T(8,128)(2,1)S(1)}, u32[]{:S(2)}, u32[]{:S(2)}) collective-permute-start(bf16[1,512,128]{2,1,0:T(8,128)(2,1)S(1)} %get-tuple-element.76), channel_id=1, source_target_pairs={{0,1},{1,2},{2,3},{3,4},{4,5},{5,6},{6,7},{7,8},{8,9},{9,10},{10,1... | collective-permute-start | bytes 393224 | tf_op jit(solution)/shard_map/ppermute | solution.py:19
  28.2 9.9 %collective-permute-start.3 = (bf16[1,512,128]{2,1,0:T(8,128)(2,1)S(1)}, bf16[1,512,128]{2,1,0:T(8,128)(2,1)S(1)}, u32[]{:S(2)}, u32[]{:S(2)}) collective-permute-start(bf16[1,512,128]{2,1,0:T(8,128)(2,1)S(1)} %get-tuple-element.77), channel_id=1, source_target_pairs={{1,0},{2,1},{3,2},{4,3},{5,4},{6,5},{7,6},{8,7},{9,8},{10,9},{11,1... | collective-permute-start | bytes 393224 | tf_op jit(solution)/shard_map/ppermute | solution.py:21
  41.4 2.6 copy-start.13
  42.7 1.3 copy-start.2
  44.0 1.6 copy-start.11
  220.1 9.7 %copy-start.5 = (bf16[8,512,128]{2,1,0:T(8,128)(2,1)S(1)}, bf16[8,512,128]{2,1,0:T(8,128)(2,1)}, u32[]{:S(2)}) copy-start(bf16[8,512,128]{2,1,0:T(8,128)(2,1)} %multiply_convert_fusion) | copy-start | bytes 3145732
  220.1 9.7 %copy-start.9 = (bf16[128,128]{1,0:T(8,128)(2,1)S(1)}, bf16[128,128]{1,0:T(8,128)(2,1)}, u32[]{:S(2)}) copy-start(bf16[128,128]{1,0:T(8,128)(2,1)} %param.18) | copy-start | bytes 98308
  220.4 11.3 %collective-permute-start.4 = (bf16[2,1,512,128]{3,2,1,0:T(8,128)(2,1)S(1)}, bf16[2,1,512,128]{3,2,1,0:T(8,128)(2,1)S(1)}, u32[]{:S(2)}, u32[]{:S(2)}) collective-permute-start(bf16[2,1,512,128]{3,2,1,0:T(8,128)(2,1)S(1)} %get-tuple-element.74), channel_id=1, source_target_pairs={{0,1},{1,2},{2,3},{3,4},{4,5},{5,6},{6,7},{7,8},{8,9},{9,10},{10,1... | collective-permute-start | bytes 786440 | tf_op jit(solution)/shard_map/ppermute | solution.py:19
  222.3 11.1 %collective-permute-start.5 = (bf16[2,1,512,128]{3,2,1,0:T(8,128)(2,1)S(1)}, bf16[2,1,512,128]{3,2,1,0:T(8,128)(2,1)S(1)}, u32[]{:S(2)}, u32[]{:S(2)}) collective-permute-start(bf16[2,1,512,128]{3,2,1,0:T(8,128)(2,1)S(1)} %get-tuple-element.75), channel_id=1, source_target_pairs={{1,0},{2,1},{3,2},{4,3},{5,4},{6,5},{7,6},{8,7},{9,8},{10,9},{11,1... | collective-permute-start | bytes 786440 | tf_op jit(solution)/shard_map/ppermute | solution.py:21
  233.8 2.4 copy-start.10
  251.1 1.0 copy-start.4
  267.3 1.0 copy-start.4
  283.4 1.0 copy-start.4
  299.6 1.0 copy-start.4
  315.7 1.0 copy-start.4
  331.9 1.0 copy-start.4
  348.0 1.0 copy-start.4
  364.1 1.0 copy-start.4
  367.6 2.4 copy-start.3
  367.6 2.4 copy-start.12
  370.0 3.0 copy-start.1
Sparse Core Ops, SparseCore 0:
  45.7 169.9 all-gather.2
where the time goes:
time: 382 us; the launch traced here: 380 us
  waiting for transfers between devices  176 us (46%)
  matrix products  81.6 us (21%)
  local copies, waits for them, and re-layouts  32.7 us (9%)
  starting transfers between devices  28.6 us (7%)
  other arithmetic  25.3 us (7%)
  loops' own time  21.9 us (6%)
  between operations  13.7 us (4%)
    all_gather x1, waiting for transfers between devices, route_pair(): every_view = lax.all_gather(normed_rows[None], 'view', axis=0, tiled=True)  170 us
    dot_general x16, matrix products, attend_row(): jnp.dot(blended, out_weight, preferred_element_type=jnp.float32)  40.5 us
    dot_general x16, matrix products, attend_row(): lax.dot_general(query_row, key_window[partner], (((1,), (1,)), ((), ())),...  25.1 us
    ppermute x3, starting transfers between devices, extended(): lax.ppermute(head, axis, [((i + 1) % count, i) for i in range(ends)])  22.9 us
    another operation x1, loops' own time, per_device(): messages = lax.map(attend_row, jnp.arange(row_count, dtype=jnp.int32))  21.9 us
    slice x8, local copies, waits for them, and re-layouts, attend_row(): value_window[partner]  18.9 us
    dot_general x18, matrix products, convolve(): jnp.dot(window.reshape(-1, channels), kernel[row_tap, col_tap], preferred...  9.82 us
    reduce_sum x16, other arithmetic, attend_row(): jnp.sum(lifted, axis=-1, keepdims=True)  9.08 us
  transfers between devices with their start and end apart: 7, of which 6 were waited for; matrix products, arithmetic and copies ran while one was open for 1% of the time, Pallas kernels for 0%

commit v1 on v0

v1 whole, which is shorter than its diff:
```python
import functools
import math

import jax
import jax.numpy as jnp
from jax import lax
from jax.experimental import pallas as pl
from jax.experimental.pallas import tpu as pltpu
from jax.sharding import PartitionSpec as P

MESH = pl.DeviceIdType.MESH
epsilon = 1e-06
ROW_STARTS = (2, 4, 6, 0)


def kernel(
    views,
    bands,
    feat_ref,
    temper_ref,
    partners_ref,
    conv_one_ref,
    conv_two_ref,
    query_w_ref,
    key_w_ref,
    value_w_ref,
    out_w_ref,
    norm_gain_ref,
    message_gain_ref,
    out_ref,
    state,
    taps_one,
    taps_two,
    kernel_one,
    kernel_two,
    kv_w,
    out_w2,
    halo_send_one,
    halo_recv_one,
    halo_send_two,
    halo_recv_two,
    normed,
    gather_a,
    gather_b,
    gather_c,
    gather_d,
    deal,
    pair,
    query,
    keys,
    values,
    temper_wide,
    scores,
    shares,
    load_sem,
    halo_ssem,
    halo_rsem,
    one_ssem,
    one_rsem,
    two_ssem,
    two_rsem,
    edge_ssem,
    edge_rsem,
):
    rows, columns, channels = state.shape
    chunk = columns // views
    view = lax.axis_index("view")
    band = lax.axis_index("band")
    up = lax.rem(band + bands - 1, bands)
    down = lax.rem(band + 1, bands)
    gathers = (gather_a, gather_b, gather_c, gather_d)

    def other(k):
        return lax.rem(view + k, views)

    spans = ((0, 1), (rows - 1, 1), (1, rows - 2))
    loads = [
        pltpu.make_async_copy(
            feat_ref.at[0, pl.ds(s, n)], state.at[pl.ds(s, n)], load_sem.at[i]
        )
        for i, (s, n) in enumerate(spans)
    ]
    for load in loads:
        load.start()
    barrier = pltpu.get_barrier_semaphore()
    for k in range(1, views):
        pl.semaphore_signal(barrier, inc=1, device_id={"view": other(k)}, device_id_type=MESH)
    for near in (up, down):
        pl.semaphore_signal(barrier, inc=1, device_id={"band": near}, device_id_type=MESH)

    def silu(x):
        return x / (1.0 + jnp.exp(-x))

    place = lax.broadcasted_iota(jnp.int32, (columns, channels), 0)

    def store_taps(taps, row, x):
        before = jnp.where(place == 0, 0.0, pltpu.roll(x, 1, 0))
        after = jnp.where(place == columns - 1, 0.0, pltpu.roll(x, columns - 1, 0))
        taps[row, :, 0:channels] = before.astype(jnp.bfloat16)
        taps[row, :, channels : 2 * channels] = x.astype(jnp.bfloat16)
        taps[row, :, 2 * channels : 3 * channels] = after.astype(jnp.bfloat16)

    def halo_copy(stage, side, send, recv):
        return pltpu.make_async_remote_copy(
            src_ref=send.at[side],
            dst_ref=recv.at[side],
            send_sem=halo_ssem.at[stage, side],
            recv_sem=halo_rsem.at[stage, side],
            device_id={"band": down if side == 0 else up},
            device_id_type=MESH,
        )

    def edge_taps(taps, recv):
        above = recv[0].astype(jnp.float32)
        store_taps(taps, 0, jnp.where(band == 0, 0.0, above))
        below = recv[1].astype(jnp.float32)
        store_taps(taps, rows + 1, jnp.where(band == bands - 1, 0.0, below))

    def conv_pair(taps, weights, first):
        wide = jnp.concatenate([taps[first + i] for i in range(4)], axis=1)
        return jnp.dot(wide, weights[...], preferred_element_type=jnp.float32)

    loads[0].wait()
    loads[1].wait()
    for row, side in ((0, 1), (rows - 1, 0)):
        x = silu(state[row])
        halo_send_one[side] = x.astype(jnp.bfloat16)
        store_taps(taps_one, row + 1, x)
    pl.semaphore_wait(barrier, views + 1)
    for side in range(2):
        halo_copy(0, side, halo_send_one, halo_recv_one).start()

    for source, target in ((conv_one_ref, kernel_one), (conv_two_ref, kernel_two)):
        for i in range(4):
            for b in range(3):
                at = (i * 3 + b) * channels
                for o in range(2):
                    if 0 <= i - o <= 2:
                        block = source[i - o, b]
                    else:
                        block = jnp.zeros((channels, channels), jnp.bfloat16)
                    target[at : at + channels, o * channels : (o + 1) * channels] = block
    kv_w[:, 0:channels] = key_w_ref[...]
    kv_w[:, channels : 2 * channels] = value_w_ref[...]
    out_w2[0:channels, :] = out_w_ref[...]
    out_w2[channels : 2 * channels, :] = out_w_ref[...]

    loads[2].wait()

    def silu_row(row, _):
        store_taps(taps_one, row + 1, silu(state[row]))
        return 0

    lax.fori_loop(1, rows - 1, silu_row, 0)

    def conv_one_step(step, _):
        first = lax.rem(2 + 2 * step, rows)

        @pl.when(step == 2)
        def _():
            for side in range(2):
                halo_copy(0, side, halo_send_one, halo_recv_one).wait_recv()
            edge_taps(taps_one, halo_recv_one)

        added = conv_pair(taps_one, kernel_one, first)
        for o in range(2):
            x = state[first + o] + added[:, o * channels : (o + 1) * channels]
            state[first + o] = x
            store_taps(taps_two, first + o + 1, silu(x))

        return 0

    lax.fori_loop(0, 4, conv_one_step, 0)
    halo_send_two[0] = taps_two[rows, :, channels : 2 * channels]
    halo_send_two[1] = taps_two[1, :, channels : 2 * channels]
    for side in range(2):
        halo_copy(1, side, halo_send_two, halo_recv_two).start()

    def one_copy(g, k):
        first = ROW_STARTS[g]
        return pltpu.make_async_remote_copy(
            src_ref=normed.at[pl.ds(first, 2), pl.ds(pl.multiple_of(other(k) * chunk, chunk), chunk)],
            dst_ref=gathers[g].at[view],
            send_sem=one_ssem.at[g, k],
            recv_sem=one_rsem.at[g, view],
            device_id={"view": other(k)},
            device_id_type=MESH,
        )

    def one_arrival(g, k):
        return pltpu.make_async_remote_copy(
            src_ref=gathers[g].at[other(k)],
            dst_ref=gathers[g].at[other(k)],
            send_sem=one_ssem.at[g, k],
            recv_sem=one_rsem.at[g, other(k)],
            device_id={"view": other(k)},
            device_id_type=MESH,
        )

    def conv_two_step(step, _):
        first = lax.rem(2 + 2 * step, rows)

        @pl.when(step == 2)
        def _():
            for side in range(2):
                halo_copy(1, side, halo_send_two, halo_recv_two).wait_recv()
            edge_taps(taps_two, halo_recv_two)

        added = conv_pair(taps_two, kernel_two, first)
        for o in range(2):
            x = state[first + o] + added[:, o * channels : (o + 1) * channels]
            state[first + o] = x
            scale = lax.rsqrt(jnp.mean(x * x, axis=-1, keepdims=True) + epsilon)
            normed[first + o] = (x * scale * norm_gain_ref[...]).astype(jnp.bfloat16)

        for g in range(4):

            @pl.when(step == g)
            def _():
                for k in range(1, views):
                    one_copy(g, k).start()

        return 0

    lax.fori_loop(0, 4, conv_two_step, 0)

    own = pl.ds(pl.multiple_of(view * chunk, chunk), chunk)

    def two_copy(g, k):
        first = ROW_STARTS[g]
        return pltpu.make_async_remote_copy(
            src_ref=deal.at[g, k],
            dst_ref=pair.at[:, pl.ds(first + 1, 2), own],
            send_sem=two_ssem.at[g, k],
            recv_sem=two_rsem.at[g, view],
            device_id={"view": other(k)},
            device_id_type=MESH,
        )

    def two_arrival(g, k):
        first = ROW_STARTS[g]
        theirs = pl.ds(pl.multiple_of(other(k) * chunk, chunk), chunk)
        return pltpu.make_async_remote_copy(
            src_ref=deal.at[g, k],
            dst_ref=pair.at[:, pl.ds(first + 1, 2), theirs],
            send_sem=two_ssem.at[g, k],
            recv_sem=two_rsem.at[g, other(k)],
            device_id={"view": other(k)},
            device_id_type=MESH,
        )

    for g in range(4):
        first = ROW_STARTS[g]
        gathers[g][view] = normed[pl.ds(first, 2), own]
        for k in range(1, views):
            one_arrival(g, k).wait_recv()
        for k in range(1, views):
            for p in range(2):
                deal[g, k, p] = gathers[g][partners_ref[other(k), p]]
        for k in range(1, views):
            two_copy(g, k).start()
        for p in range(2):
            pair[p, pl.ds(first + 1, 2), own] = gathers[g][partners_ref[view, p]]

    def query_row(row, _):
        query[row] = jnp.dot(
            normed[row], query_w_ref[...], preferred_element_type=jnp.float32
        ).astype(jnp.bfloat16)
        return 0

    lax.fori_loop(0, rows, query_row, 0)

    factor = 1.0 / math.sqrt(channels) * math.log2(math.e)
    for c in range(columns // 128):
        at = slice(c * 128, (c + 1) * 128)
        turned = jnp.concatenate([temper_ref[0, :, at] * factor] * (128 // rows), axis=0).T
        for row in range(rows):
            temper_wide[row, at, :] = jnp.broadcast_to(turned[:, row : row + 1], (128, channels))

    def fill_ones(row, _):
        for p in range(2):
            values[p, row, :, channels : 2 * channels] = jnp.ones(
                (columns, channels), jnp.bfloat16
            )
        return 0

    lax.fori_loop(0, rows + 2, fill_ones, 0)

    def project(row, keep=None):
        for p in range(2):
            both = jnp.dot(pair[p, row], kv_w[...], preferred_element_type=jnp.float32)
            if keep is not None:
                both = jnp.where(keep, both, 0.0)
            both = both.astype(jnp.bfloat16)
            keys[p, row] = both[:, 0:channels]
            values[p, row, :, 0:channels] = both[:, channels : 2 * channels]

    def edge_copy(side):
        source, target = ((rows, 0), (1, rows + 1))[side]
        return pltpu.make_async_remote_copy(
            src_ref=pair.at[:, source],
            dst_ref=pair.at[:, target],
            send_sem=edge_ssem.at[side],
            recv_sem=edge_rsem.at[side],
            device_id={"band": down if side == 0 else up},
            device_id_type=MESH,
        )

    def arrive(g):
        for k in range(1, views):
            two_arrival(g, k).wait_recv()
        if ROW_STARTS[g] == 0:
            edge_copy(1).start()
        if ROW_STARTS[g] == rows - 2:
            edge_copy(0).start()

        def one_row(i, _):
            project(ROW_STARTS[g] + 1 + i)
            return 0

        lax.fori_loop(0, 2, one_row, 0)

    def attend(step, _):
        late = step // 4
        row = (1 - late) * (3 + step) + late * lax.rem(14 - step, 8)

        @pl.when(step == 0)
        def _():
            arrive(0)
            arrive(1)

        @pl.when(step == 2)
        def _():
            arrive(2)

        @pl.when(step == 4)
        def _():
            arrive(3)

        @pl.when(step == 6)
        def _():
            for side in range(2):
                edge_copy(side).wait_recv()
            project(0, band > 0)
            project(rows + 1, band < bands - 1)

        temper = temper_wide[row]
        blended = []
        for p in range(2):
            peak = None
            for a in range(3):
                for j in range(columns // 256):
                    at = a * columns + j * 256
                    part = lax.dot_general(
                        query[row],
                        keys[p, row + a, j * 256 : (j + 1) * 256, :],
                        (((1,), (1,)), ((), ())),
                        preferred_element_type=jnp.float32,
                    )
                    scores[p, :, at : at + 256] = part
                    part = jnp.maximum(part[:, 0:128], part[:, 128:256])
                    peak = part if peak is None else jnp.maximum(peak, part)
            top = jnp.max(peak, axis=-1, keepdims=True) * temper
            for j in range(3 * columns // 128):
                at = slice(j * 128, (j + 1) * 128)
                lifted = jnp.exp2(scores[p, :, at] * temper - top)
                shares[p, :, at] = lifted.astype(jnp.bfloat16)
            total = None
            for a in range(3):
                part = jnp.dot(
                    shares[p, :, a * columns : (a + 1) * columns],
                    values[p, row + a],
                    preferred_element_type=jnp.float32,
                )
                total = part if total is None else total + part
            blended.append((total[:, 0:channels] / total[:, channels:]).astype(jnp.bfloat16))
        message = jnp.dot(
            jnp.concatenate(blended, axis=1), out_w2[...], preferred_element_type=jnp.float32
        )
        scale = lax.rsqrt(jnp.mean(message * message, axis=-1, keepdims=True) + epsilon)
        out_ref[0, row] = state[row] + message * scale * message_gain_ref[...]
        return 0

    lax.fori_loop(0, rows, attend, 0)

    for side in range(2):
        halo_copy(0, side, halo_send_one, halo_recv_one).wait_send()
        halo_copy(1, side, halo_send_two, halo_recv_two).wait_send()
        edge_copy(side).wait_send()
    for g in range(4):
        for k in range(1, views):
            one_copy(g, k).wait_send()
            two_copy(g, k).wait_send()


def per_device(views, bands, features, tempers, partners, *weights):
    conv_one, conv_two, query_w, key_w, value_w, out_w, norm_gain, message_gain = weights
    _, rows, columns, channels = features.shape
    chunk = columns // views
    half = jnp.bfloat16
    full = jnp.float32
    any_space = pl.BlockSpec(memory_space=pl.ANY)
    vmem = pl.BlockSpec(memory_space=pltpu.VMEM)
    smem = pl.BlockSpec(memory_space=pltpu.SMEM)
    dma = pltpu.SemaphoreType.DMA
    line = (columns, channels)
    return pl.pallas_call(
        functools.partial(kernel, views, bands),
        out_shape=jax.ShapeDtypeStruct(features.shape, full),
        in_specs=[any_space, vmem, smem] + [vmem] * 8,
        out_specs=vmem,
        scratch_shapes=[
            pltpu.VMEM((rows,) + line, full),
            pltpu.VMEM((rows + 2, columns, 3 * channels), half),
            pltpu.VMEM((rows + 2, columns, 3 * channels), half),
            pltpu.VMEM((12 * channels, 2 * channels), half),
            pltpu.VMEM((12 * channels, 2 * channels), half),
            pltpu.VMEM((channels, 2 * channels), half),
            pltpu.VMEM((2 * channels, channels), half),
            pltpu.VMEM((2,) + line, half),
            pltpu.VMEM((2,) + line, half),
            pltpu.VMEM((2,) + line, half),
            pltpu.VMEM((2,) + line, half),
            pltpu.VMEM((rows,) + line, half),
            pltpu.VMEM((views, 2, chunk, channels), half),
            pltpu.VMEM((views, 2, chunk, channels), half),
            pltpu.VMEM((views, 2, chunk, channels), half),
            pltpu.VMEM((views, 2, chunk, channels), half),
            pltpu.VMEM((4, views, 2, 2, chunk, channels), half),
            pltpu.VMEM((2, rows + 2) + line, half),
            pltpu.VMEM((rows,) + line, half),
            pltpu.VMEM((2, rows + 2) + line, half),
            pltpu.VMEM((2, rows + 2, columns, 2 * channels), half),
            pltpu.VMEM((rows,) + line, full),
            pltpu.VMEM((2, columns, 3 * columns), full),
            pltpu.VMEM((2, columns, 3 * columns), half),
            dma((3,)),
            dma((2, 2)),
            dma((2, 2)),
            dma((4, views)),
            dma((4, views)),
            dma((4, views)),
            dma((4, views)),
            dma((2,)),
            dma((2,)),
        ],
        compiler_params=pltpu.CompilerParams(
            collective_id=0, has_side_effects=True, vmem_limit_bytes=60 * 1024 * 1024
        ),
    )(
        features,
        tempers,
        partners,
        conv_one,
        conv_two,
        query_w,
        key_w,
        value_w,
        out_w,
        norm_gain.reshape(1, channels),
        message_gain.reshape(1, channels),
    )


def solution(mesh):
    whole = P()
    in_specs = (
        P("view", "band", None, None),
        P("view", "band", None),
    ) + (whole,) * 9
    return jax.shard_map(
        functools.partial(per_device, mesh.shape["view"], mesh.shape["band"]),
        mesh=mesh,
        in_specs=in_specs,
        out_specs=P("view", "band", None, None),
        check_vma=False,
    )
```

time: 382 us -> 77.4 us (0.20)
  the two profiles are of different devices: /device:TPU:6 before, /device:TPU:10 now
where the time goes in v1:
time: 77.4 us; the launch traced here: 77.2 us
  Pallas kernels  72.8 us (94%)
  local copies, waits for them, and re-layouts  4.41 us (6%)
    pallas_call x1, Pallas kernels, per_device(): pl.pallas_call(functools.partial(kernel, views, bands), out_shape=jax.Sha...  72.8 us
    unnamed x2, local copies, waits for them, and re-layouts  4.41 us

profile of v1, /device:TPU:10, one launch (start us, length us, event | category | flops | bytes accessed | tf_op | source)
XLA Modules:
  0.0 77.2 jit_solution(5575216775999343839)
XLA Ops:
  0.0 1.3 %copy.12.partners_ref = s32[8,2]{1,0:T(8,128)} copy(s32[8,2]{0,1:T(2,128)} %param.13) | data formatting | bytes 128 | tf_op args[2]
  1.3 72.8 %shard_map.109 = f32[1,8,512,128]{3,2,1,0:T(8,128)} custom-call(f32[1,8,512,128]{3,2,1,0:T(8,128)} %feat_ref.1, f32[1,8,512]{2,1,0:T(8,128)} %temper_ref.1, s32[8,2]{1,0:T(8,128)} %copy.12.partners_ref, bf16[3,3,128,128]{3,2,1,0:T(8,128)(2,1)} %conv_one_ref.1, bf16[3,3,128,128]{3,2,1,0:T(8,128)(2,1)} %conv_two_ref.1, bf16[128,128]{1,0:T(8,128)(2,1)} %query_w_ref.1, ...), custom_call_target="tpu_custom_call" | custom-call | tf_op jit(solution)/shard_map/pallas_call | solution.py:407
  74.1 3.1 %copy.14 = f32[1,8,512,128]{3,2,1,0:T(8,128)} copy(f32[1,8,512,128]{3,2,1,0:T(8,128)} %shard_map.109) | data formatting | bytes 4194304

commit v2 on v1

v2 whole, which is shorter than its diff:
```python
import functools
import math

import jax
import jax.numpy as jnp
from jax import lax
from jax.experimental import pallas as pl
from jax.experimental.pallas import tpu as pltpu
from jax.sharding import PartitionSpec as P

MESH = pl.DeviceIdType.MESH
epsilon = 1e-06
PAIR_STARTS = (2, 4, 0, 6)
ARRIVALS = (3, 4, 2, 5, 1, 0, 6, 7, 8, -1)
ATTENDED = (0, 0, 3, 4, 2, 1, 5, 6, 7, 0)


def kernel(
    views,
    bands,
    feat_ref,
    temper_ref,
    partners_ref,
    conv_one_ref,
    conv_two_ref,
    query_w_ref,
    key_w_ref,
    value_w_ref,
    out_w_ref,
    norm_gain_ref,
    message_gain_ref,
    out_ref,
    out_stage,
    state,
    taps_one,
    taps_two,
    kernel_one,
    kernel_two,
    query_w,
    kv_w,
    out_w2,
    halo_send_one,
    halo_recv_one,
    halo_send_two,
    halo_recv_two,
    normed,
    gather_a,
    gather_b,
    gather_c,
    gather_d,
    deal,
    pair,
    query,
    keys,
    values,
    temper_wide,
    scores,
    shares,
    load_sem,
    store_sem,
    halo_ssem,
    halo_rsem,
    one_ssem,
    one_rsem,
    two_ssem,
    two_rsem,
    edge_ssem,
    edge_rsem,
):
    rows, columns, channels = state.shape
    chunk = columns // views
    view = lax.axis_index("view")
    band = lax.axis_index("band")
    up = lax.rem(band + bands - 1, bands)
    down = lax.rem(band + 1, bands)
    strip = 32
    gathers = (gather_a, gather_b, gather_c, gather_d)

    def other(k):
        return lax.rem(view + k, views)

    barrier = pltpu.get_barrier_semaphore()
    for k in range(1, views):
        pl.semaphore_signal(barrier, inc=1, device_id={"view": other(k)}, device_id_type=MESH)
    for near in (up, down):
        pl.semaphore_signal(barrier, inc=1, device_id={"band": near}, device_id_type=MESH)
    routes = [
        (feat_ref.at[0, pl.ds(0, 1)], state.at[pl.ds(0, 1)]),
        (feat_ref.at[0, pl.ds(rows - 1, 1)], state.at[pl.ds(rows - 1, 1)]),
        (feat_ref.at[0, pl.ds(1, rows - 2)], state.at[pl.ds(1, rows - 2)]),
    ]
    for source, target in ((conv_one_ref, kernel_one), (conv_two_ref, kernel_two)):
        for a in range(3):
            for o in range(2):
                block = (pl.ds((a + o) * 3 * channels, 3 * channels), pl.ds(o * channels, channels))
                routes.append((source.at[a], target.at[block]))
    routes.append((key_w_ref, kv_w.at[:, pl.ds(0, channels)]))
    routes.append((value_w_ref, kv_w.at[:, pl.ds(channels, channels)]))
    routes.append((out_w_ref, out_w2.at[pl.ds(0, channels)]))
    routes.append((out_w_ref, out_w2.at[pl.ds(channels, channels)]))
    routes.append((query_w_ref, query_w))
    loads = [
        pltpu.make_async_copy(source, target, load_sem.at[i])
        for i, (source, target) in enumerate(routes)
    ]
    for load in loads:
        load.start()
    for target in (kernel_one, kernel_two):
        blank = jnp.zeros((3 * channels, channels), jnp.bfloat16)
        target[9 * channels : 12 * channels, 0:channels] = blank
        target[0 : 3 * channels, channels : 2 * channels] = blank

    def silu(x):
        half = 0.5 * x
        return half + half * jnp.tanh(half)

    place = lax.broadcasted_iota(jnp.int32, (columns, channels), 0)

    def store_taps(taps, row, x):
        before = jnp.where(place == 0, 0.0, pltpu.roll(x, 1, 0))
        after = jnp.where(place == columns - 1, 0.0, pltpu.roll(x, columns - 1, 0))
        taps[row, :, 0:channels] = before.astype(jnp.bfloat16)
        taps[row, :, channels : 2 * channels] = x.astype(jnp.bfloat16)
        taps[row, :, 2 * channels : 3 * channels] = after.astype(jnp.bfloat16)

    def halo_copy(stage, side, send, recv):
        return pltpu.make_async_remote_copy(
            src_ref=send.at[side],
            dst_ref=recv.at[side],
            send_sem=halo_ssem.at[stage, side],
            recv_sem=halo_rsem.at[stage, side],
            device_id={"band": down if side == 0 else up},
            device_id_type=MESH,
        )

    def edge_taps(taps, recv):
        above = recv[0].astype(jnp.float32)
        store_taps(taps, 0, jnp.where(band == 0, 0.0, above))
        below = recv[1].astype(jnp.float32)
        store_taps(taps, rows + 1, jnp.where(band == bands - 1, 0.0, below))

    def conv_pair(taps, weights, first):
        wide = jnp.concatenate([taps[first + i] for i in range(4)], axis=1)
        return jnp.dot(wide, weights[...], preferred_element_type=jnp.float32)

    loads[0].wait()
    loads[1].wait()
    for row, side in ((0, 1), (rows - 1, 0)):
        x = silu(state[row])
        halo_send_one[side] = x.astype(jnp.bfloat16)
        store_taps(taps_one, row + 1, x)
    pl.semaphore_wait(barrier, views + 1)
    for side in range(2):
        halo_copy(0, side, halo_send_one, halo_recv_one).start()

    loads[2].wait()

    def silu_row(row, _):
        store_taps(taps_one, row + 1, silu(state[row]))
        return 0

    lax.fori_loop(1, rows - 1, silu_row, 0)

    for load in loads[3:9]:
        load.wait()

    def finish_one(row, added):
        x = state[row] + added
        state[row] = x
        store_taps(taps_two, row + 1, silu(x))

    def conv_one_step(step, _):
        first = 1 + 2 * step
        added = conv_pair(taps_one, kernel_one, first)
        for o in range(2):
            finish_one(first + o, added[:, o * channels : (o + 1) * channels])
        return 0

    lax.fori_loop(0, rows // 2 - 1, conv_one_step, 0)

    def one_copy(g, k):
        first = PAIR_STARTS[g]
        return pltpu.make_async_remote_copy(
            src_ref=normed.at[pl.ds(first, 2), pl.ds(pl.multiple_of(other(k) * chunk, chunk), chunk)],
            dst_ref=gathers[g].at[view],
            send_sem=one_ssem.at[g, k],
            recv_sem=one_rsem.at[g, view],
            device_id={"view": other(k)},
            device_id_type=MESH,
        )

    def one_arrival(g, k):
        return pltpu.make_async_remote_copy(
            src_ref=gathers[g].at[other(k)],
            dst_ref=gathers[g].at[other(k)],
            send_sem=one_ssem.at[g, k],
            recv_sem=one_rsem.at[g, other(k)],
            device_id={"view": other(k)},
            device_id_type=MESH,
        )

    def conv_two_pair(first):
        added = conv_pair(taps_two, kernel_two, first)
        for o in range(2):
            x = state[first + o] + added[:, o * channels : (o + 1) * channels]
            state[first + o] = x
            scale = lax.rsqrt(jnp.mean(x * x, axis=-1, keepdims=True) + epsilon)
            normed[first + o] = (x * scale * norm_gain_ref[...]).astype(jnp.bfloat16)

    def scatter(g):
        for k in range(1, views):
            one_copy(g, k).start()

    for load in loads[9:15]:
        load.wait()

    def conv_two_inner(step, _):
        conv_two_pair(2 + 2 * step)
        for g in range(2):

            @pl.when(step == g)
            def _():
                scatter(g)

        return 0

    lax.fori_loop(0, 2, conv_two_inner, 0)

    for side in range(2):
        halo_copy(0, side, halo_send_one, halo_recv_one).wait_recv()
    edge_taps(taps_one, halo_recv_one)

    def conv_one_edge(step, _):
        row = (rows - 1) * step
        wide = jnp.concatenate([taps_one[row + i] for i in range(3)], axis=1)
        finish_one(
            row,
            jnp.dot(
                wide,
                kernel_one[0 : 9 * channels, 0:channels],
                preferred_element_type=jnp.float32,
            ),
        )
        return 0

    lax.fori_loop(0, 2, conv_one_edge, 0)
    halo_send_two[0] = taps_two[rows, :, channels : 2 * channels]
    halo_send_two[1] = taps_two[1, :, channels : 2 * channels]
    for side in range(2):
        halo_copy(1, side, halo_send_two, halo_recv_two).start()

    for load in loads[15:]:
        load.wait()
    factor = 1.0 / math.sqrt(channels) * math.log2(math.e)
    for c in range(columns // 128):
        at = slice(c * 128, (c + 1) * 128)
        turned = jnp.concatenate([temper_ref[0, :, at] * factor] * (128 // rows), axis=0).T
        for row in range(rows):
            temper_wide[row, at, :] = jnp.broadcast_to(turned[:, row : row + 1], (128, channels))

    def fill_ones(row, _):
        for p in range(2):
            at = pl.ds(pl.multiple_of(row * columns, columns), columns)
            values[p, at, channels : 2 * channels] = jnp.ones((columns, channels), jnp.bfloat16)
        return 0

    lax.fori_loop(0, rows + 2, fill_ones, 0)

    own = pl.ds(pl.multiple_of(view * chunk, chunk), chunk)

    def two_copy(row, k):
        return pltpu.make_async_remote_copy(
            src_ref=deal.at[row, k],
            dst_ref=pair.at[:, row + 1, own],
            send_sem=two_ssem.at[row, k],
            recv_sem=two_rsem.at[row, view],
            device_id={"view": other(k)},
            device_id_type=MESH,
        )

    def two_arrival(row, k):
        theirs = pl.ds(pl.multiple_of(other(k) * chunk, chunk), chunk)
        return pltpu.make_async_remote_copy(
            src_ref=deal.at[row, k],
            dst_ref=pair.at[:, row + 1, theirs],
            send_sem=two_ssem.at[row, k],
            recv_sem=two_rsem.at[row, other(k)],
            device_id={"view": other(k)},
            device_id_type=MESH,
        )

    def gathered(g):
        gathers[g][view] = normed[pl.ds(PAIR_STARTS[g], 2), own]
        for k in range(1, views):
            one_arrival(g, k).wait_recv()

    def deal_row(row):
        g = PAIR_STARTS.index(row - row % 2)
        for k in range(1, views):
            for p in range(2):
                deal[row, k, p] = gathers[g][partners_ref[p, other(k)], row % 2]
        for p in range(2):
            pair[p, row + 1, own] = gathers[g][partners_ref[p, view], row % 2]
        for k in range(1, views):
            two_copy(row, k).start()

    gathered(0)
    deal_row(3)

    for side in range(2):
        halo_copy(1, side, halo_send_two, halo_recv_two).wait_recv()
    edge_taps(taps_two, halo_recv_two)

    def conv_two_edge(step, _):
        conv_two_pair((rows - 2) * step)
        return 0

    lax.fori_loop(0, 2, conv_two_edge, 0)

    gathered(1)
    deal_row(4)
    deal_row(2)
    scatter(2)
    deal_row(5)
    scatter(3)

    def query_row(row, _):
        query[row] = jnp.dot(
            normed[row], query_w[...], preferred_element_type=jnp.float32
        ).astype(jnp.bfloat16)
        return 0

    lax.fori_loop(0, rows, query_row, 0)

    def edge_copy(side):
        source, target = ((rows, 0), (1, rows + 1))[side]
        return pltpu.make_async_remote_copy(
            src_ref=pair.at[:, source],
            dst_ref=pair.at[:, target],
            send_sem=edge_ssem.at[side],
            recv_sem=edge_rsem.at[side],
            device_id={"band": down if side == 0 else up},
            device_id_type=MESH,
        )

    def pick(table, step):
        packed = sum(entry << (4 * n) for n, entry in enumerate(table[:7]))
        rest = sum(entry << (4 * n) for n, entry in enumerate(table[7:]))
        late = step // 7
        word = (1 - late) * packed + late * rest
        return lax.shift_right_logical(word, 4 * (step - 7 * late)) % 16

    def store_out(row):
        return pltpu.make_async_copy(out_stage.at[row], out_ref.at[0, row], store_sem.at[row])

    def attend(step, _):
        row = pick(ATTENDED, step)
        place_in = pick([r + 1 for r in ARRIVALS], step)
        for n, r in enumerate(ARRIVALS):

            @pl.when(step == n)
            def _(n=n, r=r):
                if n == 3:
                    gathered(2)
                    deal_row(1)
                    deal_row(0)
                if n == 4:
                    gathered(3)
                    deal_row(6)
                    deal_row(7)
                if 0 <= r < rows:
                    for k in range(1, views):
                        two_arrival(r, k).wait_recv()
                    if r == 0:
                        edge_copy(1).start()
                    if r == rows - 1:
                        edge_copy(0).start()
                else:
                    side = 1 if r == rows else 0
                    edge_copy(side).wait_recv()
                    outside = (band == bands - 1) if side == 1 else (band == 0)

                    @pl.when(outside)
                    def _():
                        pair[:, r + 1] = jnp.zeros((2, columns, channels), jnp.bfloat16)

        for p in range(2):
            both = jnp.dot(pair[p, place_in], kv_w[...], preferred_element_type=jnp.float32)
            both = both.astype(jnp.bfloat16)
            at = pl.ds(pl.multiple_of(place_in * columns, columns), columns)
            keys[p, at] = both[:, 0:channels]
            values[p, at, 0:channels] = both[:, channels : 2 * channels]

        @pl.when(step >= 2)
        def _():
            attend_row(row)
            store_out(row).start()

        return 0

    def attend_row(row):
        blended = []
        window = pl.ds(pl.multiple_of(row * columns, columns), 3 * columns)
        for p in range(2):
            scores[p] = lax.dot_general(
                query[row],
                keys[p, window],
                (((1,), (1,)), ((), ())),
                preferred_element_type=jnp.float32,
            )
        for p in range(2):
            for k in range(columns // strip):
                at = slice(k * strip, (k + 1) * strip)
                temper = temper_wide[row, at]
                lanes = range(3 * columns // 128)
                parts = [scores[p, at, j * 128 : (j + 1) * 128] for j in lanes]
                peak = functools.reduce(jnp.maximum, parts)
                top = jnp.max(peak, axis=-1, keepdims=True) * temper
                for j in lanes:
                    lifted = jnp.exp2(parts[j] * temper - top)
                    shares[p, at, j * 128 : (j + 1) * 128] = lifted.astype(jnp.bfloat16)
            total = jnp.dot(shares[p], values[p, window], preferred_element_type=jnp.float32)
            blended.append((total[:, 0:channels] / total[:, channels:]).astype(jnp.bfloat16))
        message = jnp.dot(
            jnp.concatenate(blended, axis=1), out_w2[...], preferred_element_type=jnp.float32
        )
        scale = lax.rsqrt(jnp.mean(message * message, axis=-1, keepdims=True) + epsilon)
        out_stage[row] = state[row] + message * scale * message_gain_ref[...]

    lax.fori_loop(0, rows + 2, attend, 0)

    for side in range(2):
        halo_copy(0, side, halo_send_one, halo_recv_one).wait_send()
        halo_copy(1, side, halo_send_two, halo_recv_two).wait_send()
        edge_copy(side).wait_send()
    for g in range(4):
        for k in range(1, views):
            one_copy(g, k).wait_send()
    for row in range(rows):
        store_out(row).wait()
        for k in range(1, views):
            two_copy(row, k).wait_send()


def per_device(views, bands, features, tempers, partners, *weights):
    conv_one, conv_two, query_w, key_w, value_w, out_w, norm_gain, message_gain = weights
    _, rows, columns, channels = features.shape
    chunk = columns // views
    half = jnp.bfloat16
    full = jnp.float32
    any_space = pl.BlockSpec(memory_space=pl.ANY)
    vmem = pl.BlockSpec(memory_space=pltpu.VMEM)
    smem = pl.BlockSpec(memory_space=pltpu.SMEM)
    dma = pltpu.SemaphoreType.DMA
    line = (columns, channels)
    return pl.pallas_call(
        functools.partial(kernel, views, bands),
        out_shape=jax.ShapeDtypeStruct(features.shape, full),
        in_specs=[any_space, vmem, smem] + [any_space] * 6 + [vmem] * 2,
        out_specs=any_space,
        scratch_shapes=[
            pltpu.VMEM((rows,) + line, full),
            pltpu.VMEM((rows,) + line, full),
            pltpu.VMEM((rows + 2, columns, 3 * channels), half),
            pltpu.VMEM((rows + 2, columns, 3 * channels), half),
            pltpu.VMEM((12 * channels, 2 * channels), half),
            pltpu.VMEM((12 * channels, 2 * channels), half),
            pltpu.VMEM((channels, channels), half),
            pltpu.VMEM((channels, 2 * channels), half),
            pltpu.VMEM((2 * channels, channels), half),
            pltpu.VMEM((2,) + line, half),
            pltpu.VMEM((2,) + line, half),
            pltpu.VMEM((2,) + line, half),
            pltpu.VMEM((2,) + line, half),
            pltpu.VMEM((rows,) + line, half),
            pltpu.VMEM((views, 2, chunk, channels), half),
            pltpu.VMEM((views, 2, chunk, channels), half),
            pltpu.VMEM((views, 2, chunk, channels), half),
            pltpu.VMEM((views, 2, chunk, channels), half),
            pltpu.VMEM((rows, views, 2, chunk, channels), half),
            pltpu.VMEM((2, rows + 2) + line, half),
            pltpu.VMEM((rows,) + line, half),
            pltpu.VMEM((2, (rows + 2) * columns, channels), half),
            pltpu.VMEM((2, (rows + 2) * columns, 2 * channels), half),
            pltpu.VMEM((rows,) + line, full),
            pltpu.VMEM((2, columns, 3 * columns), full),
            pltpu.VMEM((2, columns, 3 * columns), half),
            dma((20,)),
            dma((rows,)),
            dma((2, 2)),
            dma((2, 2)),
            dma((4, views)),
            dma((4, views)),
            dma((rows, views)),
            dma((rows, views)),
            dma((2,)),
            dma((2,)),
        ],
        compiler_params=pltpu.CompilerParams(
            collective_id=0, has_side_effects=True, vmem_limit_bytes=60 * 1024 * 1024
        ),
    )(
        features,
        tempers,
        partners.T,
        conv_one.reshape(3, 3 * channels, channels),
        conv_two.reshape(3, 3 * channels, channels),
        query_w,
        key_w,
        value_w,
        out_w,
        norm_gain.reshape(1, channels),
        message_gain.reshape(1, channels),
    )


def solution(mesh):
    whole = P()
    in_specs = (
        P("view", "band", None, None),
        P("view", "band", None),
    ) + (whole,) * 9
    return jax.shard_map(
        functools.partial(per_device, mesh.shape["view"], mesh.shape["band"]),
        mesh=mesh,
        in_specs=in_specs,
        out_specs=P("view", "band", None, None),
        check_vma=False,
    )
```

time: 77.4 us -> 67.8 us (0.88); the launches traced: 77.2 us -> 66.5 us
  Pallas kernels: 72.8 us -> 63.4 us
  local copies, waits for them, and re-layouts: 4.41 us -> 3.06 us
    pallas_call x1, Pallas kernels: 72.8 us -> 63.4 us  [per_device(): pl.pallas_call(functools.partial(kernel, views, bands), out_shape=jax.Sha...]
    unnamed x2 -> x1, local copies, waits for them, and re-layouts: 4.41 us -> 3.06 us
where the time goes in v2:
time: 67.8 us; the launch traced here: 66.5 us
  Pallas kernels  63.4 us (94%)
  local copies, waits for them, and re-layouts  3.06 us (5%)
    pallas_call x1, Pallas kernels, per_device(): pl.pallas_call(functools.partial(kernel, views, bands), out_shape=jax.Sha...  63.4 us
    unnamed x1, local copies, waits for them, and re-layouts  3.06 us

profile of v2, /device:TPU:10, one launch (start us, length us, event | category | flops | bytes accessed | tf_op | source)
XLA Modules:
  0.0 66.5 jit_solution(819803366645941045)
XLA Ops:
  0.0 63.4 %shard_map.109 = f32[1,8,512,128]{3,2,1,0:T(8,128)} custom-call(f32[1,8,512,128]{3,2,1,0:T(8,128)} %feat_ref.1, f32[1,8,512]{2,1,0:T(8,128)} %temper_ref.1, s32[2,8]{1,0:T(2,128)} %bitcast.7, bf16[3,384,128]{2,1,0:T(8,128)(2,1)} %bitcast.5, bf16[3,384,128]{2,1,0:T(8,128)(2,1)} %bitcast.6, bf16[128,128]{1,0:T(8,128)(2,1)} %query_w_ref.1, ...), custom_call_target="tpu_custom_call" | custom-call | tf_op jit(solution)/shard_map/pallas_call | solution.py:456
  63.4 3.1 %copy.13 = f32[1,8,512,128]{3,2,1,0:T(8,128)} copy(f32[1,8,512,128]{3,2,1,0:T(8,128)} %shard_map.109) | data formatting | bytes 4194304

commit v3 on v2

--- a/solution.py
+++ b/solution.py
@@ -30,6 +30,9 @@
     norm_gain_ref,
     message_gain_ref,
     out_ref,
+    temper_in,
+    partners_in,
+    gains,
     out_stage,
     state,
     taps_one,
@@ -99,6 +102,10 @@
     routes.append((out_w_ref, out_w2.at[pl.ds(0, channels)]))
     routes.append((out_w_ref, out_w2.at[pl.ds(channels, channels)]))
     routes.append((query_w_ref, query_w))
+    routes.append((temper_ref.at[0], temper_in))
+    routes.append((partners_ref, partners_in))
+    routes.append((norm_gain_ref, gains.at[0]))
+    routes.append((message_gain_ref, gains.at[1]))
     loads = [
         pltpu.make_async_copy(source, target, load_sem.at[i])
         for i, (source, target) in enumerate(routes)
@@ -149,10 +156,6 @@
         x = silu(state[row])
         halo_send_one[side] = x.astype(jnp.bfloat16)
         store_taps(taps_one, row + 1, x)
-    pl.semaphore_wait(barrier, views + 1)
-    for side in range(2):
-        halo_copy(0, side, halo_send_one, halo_recv_one).start()
-
     loads[2].wait()
 
     def silu_row(row, _):
@@ -205,12 +208,13 @@
             x = state[first + o] + added[:, o * channels : (o + 1) * channels]
             state[first + o] = x
             scale = lax.rsqrt(jnp.mean(x * x, axis=-1, keepdims=True) + epsilon)
-            normed[first + o] = (x * scale * norm_gain_ref[...]).astype(jnp.bfloat16)
+            normed[first + o] = (x * scale * gains[0]).astype(jnp.bfloat16)
 
     def scatter(g):
         for k in range(1, views):
             one_copy(g, k).start()
 
+    loads[22].wait()
     for load in loads[9:15]:
         load.wait()
 
@@ -220,11 +224,77 @@
 
             @pl.when(step == g)
             def _():
+                if g == 0:
+                    pl.semaphore_wait(barrier, views + 1)
+                    for side in range(2):
+                        halo_copy(0, side, halo_send_one, halo_recv_one).start()
                 scatter(g)
 
         return 0
 
     lax.fori_loop(0, 2, conv_two_inner, 0)
+
+    for load in loads[15:22] + loads[23:]:
+        load.wait()
+    factor = 1.0 / math.sqrt(channels) * math.log2(math.e)
+    for c in range(columns // 128):
+        at = slice(c * 128, (c + 1) * 128)
+        turned = jnp.concatenate([temper_in[:, at] * factor] * (128 // rows), axis=0).T
+        for row in range(rows):
+            temper_wide[row, at, :] = jnp.broadcast_to(turned[:, row : row + 1], (128, channels))
+
+    def fill_ones(row, _):
+        for p in range(2):
+            at = pl.ds(pl.multiple_of(row * columns, columns), columns)
+            values[p, at, channels : 2 * channels] = jnp.ones((columns, channels), jnp.bfloat16)
+        return 0
+
+    lax.fori_loop(0, rows + 2, fill_ones, 0)
+
+    own = pl.ds(pl.multiple_of(view * chunk, chunk), chunk)
+
+    def two_copy(row, k):
+        return pltpu.make_async_remote_copy(
+            src_ref=deal.at[row, k],
+            dst_ref=pair.at[:, row + 1, own],
+            send_sem=two_ssem.at[row, k],
+            recv_sem=two_rsem.at[row, view],
+            device_id={"view": other(k)},
+            device_id_type=MESH,
+        )
+
+    def two_arrival(row, k):
+        theirs = pl.ds(pl.multiple_of(other(k) * chunk, chunk), chunk)
+        return pltpu.make_async_remote_copy(
+            src_ref=deal.at[row, k],
+            dst_ref=pair.at[:, row + 1, theirs],
+            send_sem=two_ssem.at[row, k],
+            recv_sem=two_rsem.at[row, other(k)],
+            device_id={"view": other(k)},
+            device_id_type=MESH,
+        )
+
+    def gathered(g):
+        gathers[g][view] = normed[pl.ds(PAIR_STARTS[g], 2), own]
+        for k in range(1, views):
+            one_arrival(g, k).wait_recv()
+
+    def deal_row(row):
+        g = PAIR_STARTS.index(row - row % 2)
+        for k in range(1, views):
+            for p in range(2):
+                deal[row, k, p] = gathers[g][partners_in[p, other(k)], row % 2]
+        for p in range(2):
+            pair[p, row + 1, own] = gathers[g][partners_in[p, view], row % 2]
+        for k in range(1, views):
+            two_copy(row, k).start()
+
+    gathered(0)
+    deal_row(3)
+    gathered(1)
+    deal_row(4)
+    deal_row(2)
+    deal_row(5)
 
     for side in range(2):
         halo_copy(0, side, halo_send_one, halo_recv_one).wait_recv()
@@ -249,96 +319,37 @@
     for side in range(2):
         halo_copy(1, side, halo_send_two, halo_recv_two).start()
 
-    for load in loads[15:]:
-        load.wait()
-    factor = 1.0 / math.sqrt(channels) * math.log2(math.e)
-    for c in range(columns // 128):
-        at = slice(c * 128, (c + 1) * 128)
-        turned = jnp.concatenate([temper_ref[0, :, at] * factor] * (128 // rows), axis=0).T
-        for row in range(rows):
-            temper_wide[row, at, :] = jnp.broadcast_to(turned[:, row : row + 1], (128, channels))
-
-    def fill_ones(row, _):
-        for p in range(2):
-            at = pl.ds(pl.multiple_of(row * columns, columns), columns)
-            values[p, at, channels : 2 * channels] = jnp.ones((columns, channels), jnp.bfloat16)
-        return 0
-
-    lax.fori_loop(0, rows + 2, fill_ones, 0)
-
-    own = pl.ds(pl.multiple_of(view * chunk, chunk), chunk)
-
-    def two_copy(row, k):
-        return pltpu.make_async_remote_copy(
-            src_ref=deal.at[row, k],
-            dst_ref=pair.at[:, row + 1, own],
-            send_sem=two_ssem.at[row, k],
-            recv_sem=two_rsem.at[row, view],
-            device_id={"view": other(k)},
-            device_id_type=MESH,
-        )
-
-    def two_arrival(row, k):
-        theirs = pl.ds(pl.multiple_of(other(k) * chunk, chunk), chunk)
-        return pltpu.make_async_remote_copy(
-            src_ref=deal.at[row, k],
-            dst_ref=pair.at[:, row + 1, theirs],
-            send_sem=two_ssem.at[row, k],
-            recv_sem=two_rsem.at[row, other(k)],
-            device_id={"view": other(k)},
-            device_id_type=MESH,
-        )
-
-    def gathered(g):
-        gathers[g][view] = normed[pl.ds(PAIR_STARTS[g], 2), own]
-        for k in range(1, views):
-            one_arrival(g, k).wait_recv()
-
-    def deal_row(row):
-        g = PAIR_STARTS.index(row - row % 2)
-        for k in range(1, views):
-            for p in range(2):
-                deal[row, k, p] = gathers[g][partners_ref[p, other(k)], row % 2]
-        for p in range(2):
-            pair[p, row + 1, own] = gathers[g][partners_ref[p, view], row % 2]
-        for k in range(1, views):
-            two_copy(row, k).start()
-
-    gathered(0)
-    deal_row(3)
-
-    for side in range(2):
-        halo_copy(1, side, halo_send_two, halo_recv_two).wait_recv()
-    edge_taps(taps_two, halo_recv_two)
-
-    def conv_two_edge(step, _):
-        conv_two_pair((rows - 2) * step)
-        return 0
-
-    lax.fori_loop(0, 2, conv_two_edge, 0)
-
-    gathered(1)
-    deal_row(4)
-    deal_row(2)
-    scatter(2)
-    deal_row(5)
-    scatter(3)
-
     def query_row(row, _):
         query[row] = jnp.dot(
             normed[row], query_w[...], preferred_element_type=jnp.float32
         ).astype(jnp.bfloat16)
         return 0
 
-    lax.fori_loop(0, rows, query_row, 0)
-
-    def edge_copy(side):
+    lax.fori_loop(2, rows - 2, query_row, 0)
+
+    for side in range(2):
+        halo_copy(1, side, halo_send_two, halo_recv_two).wait_recv()
+    edge_taps(taps_two, halo_recv_two)
+
+    def conv_two_edge(step, _):
+        conv_two_pair((rows - 2) * step)
+        return 0
+
+    lax.fori_loop(0, 2, conv_two_edge, 0)
+
+    scatter(2)
+    scatter(3)
+    lax.fori_loop(0, 2, query_row, 0)
+    lax.fori_loop(rows - 2, rows, query_row, 0)
+
+    def edge_copy(side, k):
         source, target = ((rows, 0), (1, rows + 1))[side]
+        at = pl.ds(pl.multiple_of(other(k) * chunk, chunk), chunk)
         return pltpu.make_async_remote_copy(
-            src_ref=pair.at[:, source],
-            dst_ref=pair.at[:, target],
-            send_sem=edge_ssem.at[side],
-            recv_sem=edge_rsem.at[side],
+            src_ref=pair.at[:, source, at],
+            dst_ref=pair.at[:, target, at],
+            send_sem=edge_ssem.at[side, k],
+            recv_sem=edge_rsem.at[side, k],
             device_id={"band": down if side == 0 else up},
             device_id_type=MESH,
         )
@@ -369,15 +380,17 @@
                     deal_row(6)
                     deal_row(7)
                 if 0 <= r < rows:
+                    side = {0: 1, rows - 1: 0}.get(r)
+                    if side is not None:
+                        edge_copy(side, 0).start()
                     for k in range(1, views):
                         two_arrival(r, k).wait_recv()
-                    if r == 0:
-                        edge_copy(1).start()
-                    if r == rows - 1:
-                        edge_copy(0).start()
+                        if side is not None:
+                            edge_copy(side, k).start()
                 else:
                     side = 1 if r == rows else 0
-                    edge_copy(side).wait_recv()
+                    for k in range(views):
+                        edge_copy(side, k).wait_recv()
                     outside = (band == bands - 1) if side == 1 else (band == 0)
 
                     @pl.when(outside)
@@ -425,14 +438,15 @@
             jnp.concatenate(blended, axis=1), out_w2[...], preferred_element_type=jnp.float32
         )
         scale = lax.rsqrt(jnp.mean(message * message, axis=-1, keepdims=True) + epsilon)
-        out_stage[row] = state[row] + message * scale * message_gain_ref[...]
+        out_stage[row] = state[row] + message * scale * gains[1]
 
     lax.fori_loop(0, rows + 2, attend, 0)
 
     for side in range(2):
         halo_copy(0, side, halo_send_one, halo_recv_one).wait_send()
         halo_copy(1, side, halo_send_two, halo_recv_two).wait_send()
-        edge_copy(side).wait_send()
+        for k in range(views):
+            edge_copy(side, k).wait_send()
     for g in range(4):
         for k in range(1, views):
             one_copy(g, k).wait_send()
@@ -442,6 +456,23 @@
             two_copy(row, k).wait_send()
 
 
+def hand_over(source, target, stage, in_sem, out_sem):
+    count = stage.shape[0]
+    reads = [
+        pltpu.make_async_copy(source.at[0, i], stage.at[i], in_sem.at[i]) for i in range(count)
+    ]
+    writes = [
+        pltpu.make_async_copy(stage.at[i], target.at[0, i], out_sem.at[i]) for i in range(count)
+    ]
+    for read in reads:
+        read.start()
+    for read, write in zip(reads, writes):
+        read.wait()
+        write.start()
+    for write in writes:
+        write.wait()
+
+
 def per_device(views, bands, features, tempers, partners, *weights):
     conv_one, conv_two, query_w, key_w, value_w, out_w, norm_gain, message_gain = weights
     _, rows, columns, channels = features.shape
@@ -449,16 +480,17 @@
     half = jnp.bfloat16
     full = jnp.float32
     any_space = pl.BlockSpec(memory_space=pl.ANY)
-    vmem = pl.BlockSpec(memory_space=pltpu.VMEM)
-    smem = pl.BlockSpec(memory_space=pltpu.SMEM)
     dma = pltpu.SemaphoreType.DMA
     line = (columns, channels)
-    return pl.pallas_call(
+    refined = pl.pallas_call(
         functools.partial(kernel, views, bands),
         out_shape=jax.ShapeDtypeStruct(features.shape, full),
-        in_specs=[any_space, vmem, smem] + [any_space] * 6 + [vmem] * 2,
+        in_specs=[any_space] * 11,
         out_specs=any_space,
         scratch_shapes=[
+            pltpu.VMEM((rows, columns), full),
+            pltpu.SMEM((2, views), jnp.int32),
+            pltpu.VMEM((2, 1, channels), full),
             pltpu.VMEM((rows,) + line, full),
             pltpu.VMEM((rows,) + line, full),
             pltpu.VMEM((rows + 2, columns, 3 * channels), half),
@@ -485,7 +517,7 @@
             pltpu.VMEM((rows,) + line, full),
             pltpu.VMEM((2, columns, 3 * columns), full),
             pltpu.VMEM((2, columns, 3 * columns), half),
-            dma((20,)),
+            dma((24,)),
             dma((rows,)),
             dma((2, 2)),
             dma((2, 2)),
@@ -493,8 +525,8 @@
             dma((4, views)),
             dma((rows, views)),
             dma((rows, views)),
-            dma((2,)),
-            dma((2,)),
+            dma((2, views)),
+            dma((2, views)),
         ],
         compiler_params=pltpu.CompilerParams(
             collective_id=0, has_side_effects=True, vmem_limit_bytes=60 * 1024 * 1024
@@ -512,6 +544,14 @@
         norm_gain.reshape(1, channels),
         message_gain.reshape(1, channels),
     )
+    return pl.pallas_call(
+        hand_over,
+        out_shape=jax.ShapeDtypeStruct(features.shape, full),
+        in_specs=[any_space],
+        out_specs=any_space,
+        scratch_shapes=[pltpu.VMEM((rows,) + line, full), dma((rows,)), dma((rows,))],
+        compiler_params=pltpu.CompilerParams(vmem_limit_bytes=60 * 1024 * 1024),
+    )(refined)
 
 
 def solution(mesh):

time: 67.8 us -> 64 us (0.944)
  local copies, waits for them, and re-layouts: 3.06 us -> 0 us
    unnamed x1 -> x0, local copies, waits for them, and re-layouts: 3.06 us -> none
    pallas_call x1, Pallas kernels: 63.4 us -> 60.8 us  [per_device(): pl.pallas_call(functools.partial(kernel, views, bands), out_shape=jax.Sha...]
    pallas_call x0 -> x1, Pallas kernels: none -> 2.39 us  [per_device(): pl.pallas_call(hand_over, out_shape=jax.ShapeDtypeStruct(features.shape,...]
where the time goes in v3:
time: 64 us; the launch traced here: 63.2 us
  Pallas kernels  63.2 us (99%)
    pallas_call x1, Pallas kernels, per_device(): pl.pallas_call(functools.partial(kernel, views, bands), out_shape=jax.Sha...  60.8 us
    pallas_call x1, Pallas kernels, per_device(): pl.pallas_call(hand_over, out_shape=jax.ShapeDtypeStruct(features.shape,...  2.39 us

profile of v3, /device:TPU:10, one launch (start us, length us, event | category | flops | bytes accessed | tf_op | source)
XLA Modules:
  0.0 63.2 jit_solution(17020274484607969920)
XLA Ops:
  0.0 60.8 %shard_map.109.source = f32[1,8,512,128]{3,2,1,0:T(8,128)} custom-call(f32[1,8,512,128]{3,2,1,0:T(8,128)} %feat_ref.1, f32[1,8,512]{2,1,0:T(8,128)} %temper_ref.1, s32[2,8]{1,0:T(2,128)} %bitcast.7, bf16[3,384,128]{2,1,0:T(8,128)(2,1)} %bitcast.5, bf16[3,384,128]{2,1,0:T(8,128)(2,1)} %bitcast.6, bf16[128,128]{1,0:T(8,128)(2,1)} %query_w_ref.1, ...), custom_call_target="tpu_custom_call" | custom-call | tf_op jit(solution)/shard_map/pallas_call | solution.py:485
  60.8 2.4 %shard_map.110 = f32[1,8,512,128]{3,2,1,0:T(8,128)} custom-call(f32[1,8,512,128]{3,2,1,0:T(8,128)} %shard_map.109.source), custom_call_target="tpu_custom_call" | custom-call | tf_op jit(solution)/shard_map/pallas_call | solution.py:547

commit v4 on v3

--- a/solution.py
+++ b/solution.py
@@ -78,6 +78,8 @@
     down = lax.rem(band + 1, bands)
     strip = 32
     gathers = (gather_a, gather_b, gather_c, gather_d)
+    leaves = (band < bands - 1, band > 0)
+    enters = (band > 0, band < bands - 1)
 
     def other(k):
         return lax.rem(view + k, views)
@@ -141,10 +143,13 @@
         )
 
     def edge_taps(taps, recv):
-        above = recv[0].astype(jnp.float32)
-        store_taps(taps, 0, jnp.where(band == 0, 0.0, above))
-        below = recv[1].astype(jnp.float32)
-        store_taps(taps, rows + 1, jnp.where(band == bands - 1, 0.0, below))
+        for side, row in ((0, 0), (1, rows + 1)):
+
+            @pl.when(jnp.logical_not(enters[side]))
+            def _():
+                recv[side] = jnp.zeros((columns, channels), jnp.bfloat16)
+
+            store_taps(taps, row, recv[side].astype(jnp.float32))
 
     def conv_pair(taps, weights, first):
         wide = jnp.concatenate([taps[first + i] for i in range(4)], axis=1)
@@ -227,7 +232,7 @@
                 if g == 0:
                     pl.semaphore_wait(barrier, views + 1)
                     for side in range(2):
-                        halo_copy(0, side, halo_send_one, halo_recv_one).start()
+                        pl.when(leaves[side])(halo_copy(0, side, halo_send_one, halo_recv_one).start)
                 scatter(g)
 
         return 0
@@ -291,13 +296,8 @@
 
     gathered(0)
     deal_row(3)
-    gathered(1)
-    deal_row(4)
-    deal_row(2)
-    deal_row(5)
-
     for side in range(2):
-        halo_copy(0, side, halo_send_one, halo_recv_one).wait_recv()
+        pl.when(enters[side])(halo_copy(0, side, halo_send_one, halo_recv_one).wait_recv)
     edge_taps(taps_one, halo_recv_one)
 
     def conv_one_edge(step, _):
@@ -317,7 +317,12 @@
     halo_send_two[0] = taps_two[rows, :, channels : 2 * channels]
     halo_send_two[1] = taps_two[1, :, channels : 2 * channels]
     for side in range(2):
-        halo_copy(1, side, halo_send_two, halo_recv_two).start()
+        pl.when(leaves[side])(halo_copy(1, side, halo_send_two, halo_recv_two).start)
+
+    gathered(1)
+    deal_row(4)
+    deal_row(2)
+    deal_row(5)
 
     def query_row(row, _):
         query[row] = jnp.dot(
@@ -328,17 +333,21 @@
     lax.fori_loop(2, rows - 2, query_row, 0)
 
     for side in range(2):
-        halo_copy(1, side, halo_send_two, halo_recv_two).wait_recv()
+        pl.when(enters[side])(halo_copy(1, side, halo_send_two, halo_recv_two).wait_recv)
     edge_taps(taps_two, halo_recv_two)
 
     def conv_two_edge(step, _):
         conv_two_pair((rows - 2) * step)
+        for g in range(2):
+
+            @pl.when(step == g)
+            def _():
+                scatter(g + 2)
+
         return 0
 
     lax.fori_loop(0, 2, conv_two_edge, 0)
 
-    scatter(2)
-    scatter(3)
     lax.fori_loop(0, 2, query_row, 0)
     lax.fori_loop(rows - 2, rows, query_row, 0)
 
@@ -382,18 +391,20 @@
                 if 0 <= r < rows:
                     side = {0: 1, rows - 1: 0}.get(r)
                     if side is not None:
-                        edge_copy(side, 0).start()
+                        pl.when(leaves[side])(edge_copy(side, 0).start)
                     for k in range(1, views):
                         two_arrival(r, k).wait_recv()
                         if side is not None:
-                            edge_copy(side, k).start()
+                            pl.when(leaves[side])(edge_copy(side, k).start)
                 else:
                     side = 1 if r == rows else 0
-                    for k in range(views):
-                        edge_copy(side, k).wait_recv()
-                    outside = (band == bands - 1) if side == 1 else (band == 0)
-
-                    @pl.when(outside)
+
+                    @pl.when(enters[side])
+                    def _():
+                        for k in range(views):
+                            edge_copy(side, k).wait_recv()
+
+                    @pl.when(jnp.logical_not(enters[side]))
                     def _():
                         pair[:, r + 1] = jnp.zeros((2, columns, channels), jnp.bfloat16)
 
@@ -443,10 +454,10 @@
     lax.fori_loop(0, rows + 2, attend, 0)
 
     for side in range(2):
-        halo_copy(0, side, halo_send_one, halo_recv_one).wait_send()
-        halo_copy(1, side, halo_send_two, halo_recv_two).wait_send()
+        pl.when(leaves[side])(halo_copy(0, side, halo_send_one, halo_recv_one).wait_send)
+        pl.when(leaves[side])(halo_copy(1, side, halo_send_two, halo_recv_two).wait_send)
         for k in range(views):
-            edge_copy(side, k).wait_send()
+            pl.when(leaves[side])(edge_copy(side, k).wait_send)
     for g in range(4):
         for k in range(1, views):
             one_copy(g, k).wait_send()

time: 64 us -> 62.1 us (0.970)
  Pallas kernels: 63.2 us -> 61.4 us
    pallas_call x1, Pallas kernels: 60.8 us -> 59 us  [per_device(): pl.pallas_call(functools.partial(kernel, views, bands), out_shape=jax.Sha...]
where the time goes in v4:
time: 62.1 us; the launch traced here: 61.4 us
  Pallas kernels  61.4 us (99%)
    pallas_call x1, Pallas kernels, per_device(): pl.pallas_call(functools.partial(kernel, views, bands), out_shape=jax.Sha...  59 us
    pallas_call x1, Pallas kernels, per_device(): pl.pallas_call(hand_over, out_shape=jax.ShapeDtypeStruct(features.shape,...  2.39 us

profile of v4, /device:TPU:10, one launch (start us, length us, event | category | flops | bytes accessed | tf_op | source)
XLA Modules:
  0.0 61.4 jit_solution(4494077258823820681)
XLA Ops:
  0.0 59.0 %shard_map.109.source = f32[1,8,512,128]{3,2,1,0:T(8,128)} custom-call(f32[1,8,512,128]{3,2,1,0:T(8,128)} %feat_ref.1, f32[1,8,512]{2,1,0:T(8,128)} %temper_ref.1, s32[2,8]{1,0:T(2,128)} %bitcast.7, bf16[3,384,128]{2,1,0:T(8,128)(2,1)} %bitcast.5, bf16[3,384,128]{2,1,0:T(8,128)(2,1)} %bitcast.6, bf16[128,128]{1,0:T(8,128)(2,1)} %query_w_ref.1, ...), custom_call_target="tpu_custom_call" | custom-call | tf_op jit(solution)/shard_map/pallas_call | solution.py:496
  59.0 2.4 %shard_map.110 = f32[1,8,512,128]{3,2,1,0:T(8,128)} custom-call(f32[1,8,512,128]{3,2,1,0:T(8,128)} %shard_map.109.source), custom_call_target="tpu_custom_call" | custom-call | tf_op jit(solution)/shard_map/pallas_call | solution.py:558
